TPU v7x, 128 devices: a whole 4x4x4 slice. The times are simulated.
128 devices in a mesh: row: 16 (over y, z), col: 8 (over x, core).
Axes of the slice: x: 4, y: 4, z: 4, core: 2. Of those that a mesh axis runs over, the one named last changes fastest.
Arguments:
- block_cols: int32 [64, 16], replicated, may hold values from -1 to 63, as said below
- step_dir: bfloat16 [64, 16, 128, 128], P('row', 'col')
- intersection: bfloat16 [64, 16, 128, 128], P('row', 'col')
- density: bfloat16 [64, 16, 128, 128], P('row', 'col')
- kohn_sham: bfloat16 [64, 16, 128, 128], P('row', 'col')
Outputs:
- commutator: bfloat16 [64, 16, 128, 128], P('row', 'col')
- trace_value: float32 [], replicated
Inputs may be any that keep to these rules, and one draw needn't show every extreme that they name: block_cols[i, s] is -1 or a block column of group s // 2, that is from (s // 2) * 8 to (s // 2 + 1) * 8 - 1; the live entries of one block row within one group are distinct; the pattern is symmetric (j is live in row i exactly when i is live in row j) and holds every diagonal block.
All inputs are finite; a program needn't handle non-finite values.
Results may differ from a plain program's by a relative error of at most 0.0057.
Values may be sent and summed in bfloat16 or wider, within the bound.
A program may use at most 64 MiB of HBM per device.

v0:
```python
import jax
import jax.numpy as jnp
from jax import lax
from jax.sharding import PartitionSpec as P


def per_device(block_cols, step_dir, intersection, density, kohn_sham):
    row_total = step_dir.shape[0]
    slot_total = step_dir.shape[1]
    block_size = step_dir.shape[2]
    col_groups = lax.axis_size("col")
    blocks_total = block_cols.shape[0]
    row_index = lax.axis_index("row")
    col_index = lax.axis_index("col")
    own_rows = lax.dynamic_slice_in_dim(block_cols, row_index * row_total, row_total, 0)
    own_cols = lax.dynamic_slice_in_dim(own_rows, col_index * slot_total, slot_total, 1)
    group_cols = lax.dynamic_slice_in_dim(block_cols, col_index * slot_total, slot_total, 1)
    left_live = own_cols >= 0
    targets = own_rows.reshape(row_total, col_groups, slot_total).transpose(1, 0, 2)

    def partial_blocks(left_blocks, gathered, wanted):
        safe_rows = jnp.clip(wanted, 0, blocks_total - 1)
        right_rows = gathered[safe_rows]
        right_cols = group_cols[safe_rows]
        matched = (
            (right_cols[:, :, :, None, :] == own_cols[None, :, None, :, None])
            & left_live[None, :, None, :, None]
            & (wanted >= 0)[:, :, :, None, None]
        )
        picked = jnp.where(
            matched[..., None, None],
            right_rows[:, :, :, None, :, :, :],
            jnp.zeros((), jnp.bfloat16),
        ).sum(axis=4)
        terms = jnp.einsum(
            "iapr,gisaqr->gispq", left_blocks, picked, preferred_element_type=jnp.float32
        )
        group_count = wanted.shape[0]
        return terms.reshape(group_count * row_total, slot_total, block_size, block_size)

    def product(left_blocks, right_blocks):
        gathered = lax.all_gather(right_blocks, "row", axis=0, tiled=True)
        return lax.psum_scatter(
            partial_blocks(left_blocks, gathered, targets), "col", scatter_dimension=0, tiled=True
        )

    scaled_step = product(step_dir, intersection).astype(jnp.bfloat16)
    change = (-(product(scaled_step, density) + product(density, scaled_step))).astype(jnp.bfloat16)
    commutator = (product(kohn_sham, change) - product(change, kohn_sham)).astype(jnp.bfloat16)
    local_trace = jnp.sum(change.astype(jnp.float32) * kohn_sham.astype(jnp.float32))
    trace_value = lax.psum(local_trace, ("row", "col")) / (blocks_total * block_size * block_size)
    return (commutator, trace_value)


def solution(mesh):
    in_specs = (
        P(),
        P("row", "col", None, None),
        P("row", "col", None, None),
        P("row", "col", None, None),
        P("row", "col", None, None),
    )
    out_specs = (P("row", "col", None, None), P())
    return jax.shard_map(
        per_device, mesh=mesh, in_specs=in_specs, out_specs=out_specs, check_vma=False
    )
```

profile of v0, /device:TPU:39, one launch (start us, length us, event | category | flops | bytes accessed | tf_op | source)
XLA Modules:
  0.0 498.7 jit_solution(6847474959793263105)
XLA Ops:
  7.2 0.0 copy-start
  7.2 0.0 all-gather.14.cloned.1.call-start
  7.2 0.7 all-gather.14.cloned.1.call-update
  7.9 0.0 all-gather.8.cloned.1.call-start
  8.0 0.7 all-gather.8.cloned.1.call-update
  8.7 0.0 all-gather.6.cloned.1.call-start
  8.7 0.7 all-gather.6.cloned.1.call-update
  9.4 0.0 reduce-scatter.5.cloned.1.call-start
  9.5 0.8 broadcast_compare_fusion
  10.2 0.1 copy.44
  10.3 0.1 copy.43
  10.4 0.8 dynamic-slice_compare_fusion
  11.2 0.1 copy.45
  11.3 0.1 ge.18
  11.4 0.8 dynamic-slice_clamp_fusion
  12.2 0.1 copy.40
  12.3 0.1 reshape.45
  12.5 0.7 constant_dynamic-slice_fusion
  13.2 0.1 copy.67
  13.3 0.6 gather_fusion
  13.9 0.1 and_and_fusion
  14.0 49.2 %all-gather.14.cloned.1.call-done = bf16[64,2,128,128]{3,2,1,0:T(8,128)(2,1)} async-done(((bf16[4,2,128,128]{3,2,1,0:T(8,128)(2,1)}), bf16[64,2,128,128]{3,2,1,0:T(8,128)(2,1)}) %all-gather.14.cloned.1.call-update) | async-done | bytes 4194320 | tf_op jit(solution)/shard_map/all_gather | solution.py:42
  63.3 5.2 %gather_fusion.5 = bf16[64,2,128,128]{3,2,1,0:T(8,128)(2,1)} fusion(bf16[64,2,128,128]{3,2,1,0:T(8,128)(2,1)} %all-gather.14.cloned.1.call-done, s32[1024]{0:T(1024)S(1)} %pad_clamp_fusion), kind=kCustom, calls=%fused_computation.5 | custom fusion | bytes 8388864 | tf_op jit(solution)/shard_map/gather | solution.py:23
  68.5 48.0 %all-gather.8.cloned.1.call-done = bf16[64,2,128,128]{3,2,1,0:T(8,128)(2,1)} async-done(((bf16[4,2,128,128]{3,2,1,0:T(8,128)(2,1)}), bf16[64,2,128,128]{3,2,1,0:T(8,128)(2,1)}) %all-gather.8.cloned.1.call-update) | async-done | bytes 4194320 | tf_op jit(solution)/shard_map/all_gather | solution.py:42
  116.5 5.2 %gather_fusion.2 = bf16[64,2,128,128]{3,2,1,0:T(8,128)(2,1)} fusion(bf16[64,2,128,128]{3,2,1,0:T(8,128)(2,1)} %all-gather.8.cloned.1.call-done, s32[1024]{0:T(1024)S(1)} %pad_clamp_fusion), kind=kCustom, calls=%fused_computation.2 | custom fusion | bytes 8388864 | tf_op jit(solution)/shard_map/gather | solution.py:23
  121.7 48.1 %all-gather.6.cloned.1.call-done = bf16[64,2,128,128]{3,2,1,0:T(8,128)(2,1)} async-done(((bf16[4,2,128,128]{3,2,1,0:T(8,128)(2,1)}), bf16[64,2,128,128]{3,2,1,0:T(8,128)(2,1)}) %all-gather.6.cloned.1.call-update) | async-done | bytes 4194320 | tf_op jit(solution)/shard_map/all_gather | solution.py:42
  169.8 5.2 %gather_fusion.1 = bf16[64,2,128,128]{3,2,1,0:T(8,128)(2,1)} fusion(bf16[64,2,128,128]{3,2,1,0:T(8,128)(2,1)} %all-gather.6.cloned.1.call-done, s32[1024]{0:T(1024)S(1)} %pad_clamp_fusion), kind=kCustom, calls=%fused_computation.1 | custom fusion | bytes 8388864 | tf_op jit(solution)/shard_map/gather | solution.py:23
  175.0 17.5 %select_reduce_fusion = (bf16[8,4,2,2,128,128]{5,4,3,2,1,0:T(8,128)(2,1)}, bf16[8,4,2,2,128,128]{5,4,3,2,1,0:T(8,128)(2,1)S(1)}, bf16[8,4,2,2,128,128]{5,4,3,2,1,0:T(8,128)(2,1)}) fusion(pred[8,4,2,2,2]{4,3,2,1,0:T(4,128)(4,1)S(1)} %and_and_fusion, bf16[8,4,2,2,128,128]{5,4,3,2,1,0:T(8,128)(2,1)} %bitcast.70, bf16[8,4,2,2,128,128]{5,4,3,2,1,0:T(8,128)(2,1)} %bitcast.71, ...), kind=kLoop, calls=%fused_computation.6 | loop fusion | flops 18874368 | bytes 25166080 | tf_op jit(solution)/shard_map/reduce_sum | solution.py:34
  192.5 3.2 fusion.11
  195.7 5.4 %copy.48 = f32[8,4,2,128,128]{4,3,2,1,0:T(8,128)} copy(f32[8,4,2,128,128]{3,4,2,0,1:T(8,128)} %fusion.11) | data formatting | bytes 8388608 | tf_op jit(solution)/shard_map/iapr,gisaqr->gispq/transpose | solution.py:35
  201.0 0.0 reduce-scatter.5.cloned.1.call-update
  201.1 0.0 all-gather.10.cloned.1.call-start
  201.1 36.4 %reduce-scatter.5.cloned.1.call-done = f32[4,2,128,128]{3,2,1,0:T(8,128)} async-done(((f32[32,2,128,128]{3,2,1,0:T(8,128)}), f32[4,2,128,128]{3,2,1,0:T(8,128)}) %reduce-scatter.5.cloned.1.call-update) | async-done | bytes 524304 | tf_op jit(solution)/shard_map/reduce_scatter | solution.py:43
  237.5 1.8 convert_element_type.10
  239.3 0.0 all-gather.10.cloned.1.call-update
  239.3 0.2 reduce-scatter.11.cloned.1.call-start
  239.5 52.2 %all-gather.10.cloned.1.call-done = bf16[64,2,128,128]{3,2,1,0:T(8,128)(2,1)} async-done(((bf16[4,2,128,128]{3,2,1,0:T(8,128)(2,1)}), bf16[64,2,128,128]{3,2,1,0:T(8,128)(2,1)}) %all-gather.10.cloned.1.call-update) | async-done | bytes 4194320 | tf_op jit(solution)/shard_map/all_gather | solution.py:42
  291.7 5.2 %gather_fusion.3 = bf16[64,2,128,128]{3,2,1,0:T(8,128)(2,1)} fusion(bf16[64,2,128,128]{3,2,1,0:T(8,128)(2,1)} %all-gather.10.cloned.1.call-done, s32[1024]{0:T(1024)S(1)} %pad_clamp_fusion), kind=kCustom, calls=%fused_computation.3 | custom fusion | bytes 8388864 | tf_op jit(solution)/shard_map/gather | solution.py:23
  296.9 6.2 %select_reduce_fusion.2 = bf16[8,4,2,2,128,128]{5,4,3,2,1,0:T(8,128)(2,1)S(1)} fusion(pred[8,4,2,2,2]{4,3,2,1,0:T(4,128)(4,1)S(1)} %and_and_fusion, bf16[8,4,2,2,128,128]{5,4,3,2,1,0:T(8,128)(2,1)} %bitcast.69), kind=kLoop, calls=%fused_computation.8 | loop fusion | flops 6291456 | bytes 8388864 | tf_op jit(solution)/shard_map/reduce_sum | solution.py:34
  303.2 1.3 fusion.5
  304.4 0.9 copy-done.2
  305.3 0.0 copy-done.3
  305.3 3.2 fusion
  308.6 5.4 %copy.51 = f32[8,4,2,128,128]{4,3,2,1,0:T(8,128)} copy(f32[8,4,2,128,128]{3,4,2,0,1:T(8,128)} %fusion) | data formatting | bytes 8388608 | tf_op jit(solution)/shard_map/add | solution.py:48
  313.9 0.0 reduce-scatter.11.cloned.1.call-update
  314.0 0.0 all-gather.12.cloned.1.call-start
  314.0 36.4 %reduce-scatter.11.cloned.1.call-done = f32[4,2,128,128]{3,2,1,0:T(8,128)} async-done(((f32[32,2,128,128]{3,2,1,0:T(8,128)}), f32[4,2,128,128]{3,2,1,0:T(8,128)}) %reduce-scatter.11.cloned.1.call-update) | async-done | bytes 524304 | tf_op jit(solution)/shard_map/reduce_scatter | solution.py:43
  350.4 2.4 multiply_reduce_fusion
  352.8 0.0 all-gather.12.cloned.1.call-update
  352.8 0.0 reduce-scatter.9.cloned.1.call-start
  352.9 5.4 %fusion.17 = f32[8,4,2,128,128]{3,4,2,0,1:T(8,128)} fusion(bf16[8,4,2,2,128,128]{5,4,3,2,1,0:T(8,128)(2,1)} %get-tuple-element.2, bf16[4,2,128,128]{3,2,1,0:T(8,128)(2,1)} %get-tuple-element.6), kind=kOutput, calls=%fused_computation.25 | convolution fusion | flops 536870912 | bytes 8650752 | tf_op jit(solution)/shard_map/iapr,gisaqr->gispq/dot_general | solution.py:35
  358.3 5.4 %copy.55 = f32[8,4,2,128,128]{4,3,2,1,0:T(8,128)} copy(f32[8,4,2,128,128]{3,4,2,0,1:T(8,128)} %fusion.17) | data formatting | bytes 8388608 | tf_op jit(solution)/shard_map/iapr,gisaqr->gispq/transpose | solution.py:35
  363.6 0.0 reduce-scatter.9.cloned.1.call-update
  363.7 0.0 reduce-scatter.7.cloned.1.call-start
  363.7 41.1 %all-gather.12.cloned.1.call-done = bf16[64,2,128,128]{3,2,1,0:T(8,128)(2,1)} async-done(((bf16[4,2,128,128]{3,2,1,0:T(8,128)(2,1)}), bf16[64,2,128,128]{3,2,1,0:T(8,128)(2,1)}) %all-gather.12.cloned.1.call-update) | async-done | bytes 4194320 | tf_op jit(solution)/shard_map/all_gather | solution.py:42
  404.8 5.2 %gather_fusion.4 = bf16[64,2,128,128]{3,2,1,0:T(8,128)(2,1)} fusion(bf16[64,2,128,128]{3,2,1,0:T(8,128)(2,1)} %all-gather.12.cloned.1.call-done, s32[1024]{0:T(1024)S(1)} %pad_clamp_fusion), kind=kCustom, calls=%fused_computation.4 | custom fusion | bytes 8388864 | tf_op jit(solution)/shard_map/gather | solution.py:23
  410.0 6.2 %select_reduce_fusion.1 = bf16[8,4,2,2,128,128]{5,4,3,2,1,0:T(8,128)(2,1)S(1)} fusion(pred[8,4,2,2,2]{4,3,2,1,0:T(4,128)(4,1)S(1)} %and_and_fusion, bf16[8,4,2,2,128,128]{5,4,3,2,1,0:T(8,128)(2,1)} %bitcast.68), kind=kLoop, calls=%fused_computation.7 | loop fusion | flops 6291456 | bytes 8388864 | tf_op jit(solution)/shard_map/reduce_sum | solution.py:34
  416.2 3.2 fusion.14
  419.4 5.5 %copy.53 = f32[8,4,2,128,128]{4,3,2,1,0:T(8,128)} copy(f32[8,4,2,128,128]{3,4,2,0,1:T(8,128)} %fusion.14) | data formatting | bytes 8388608 | tf_op jit(solution)/shard_map/iapr,gisaqr->gispq/transpose | solution.py:35
  424.8 0.0 reduce-scatter.7.cloned.1.call-update
  424.9 63.5 %psum.7 = f32[]{:T(128)} all-reduce(f32[]{:T(128)} %get-tuple-element.5), channel_id=1, replica_groups=mesh['row'=16,'col'=8] {'row','col'}, use_global_device_ids=true, to_apply=%region_11.12 | all-reduce | flops 1 | bytes 8 | tf_op jit(solution)/shard_map/psum | solution.py:51
  489.1 0.0 reduce-scatter.9.cloned.1.call-done
  489.1 0.0 reduce-scatter.7.cloned.1.call-done
  489.1 2.0 subtract_convert_fusion
  (12 shorter events, 0.0 us)
Async XLA Ops:
  7.2 185.3 %copy-start = (bf16[4,2,128,128]{3,2,1,0:T(8,128)(2,1)S(1)}, bf16[4,2,128,128]{3,2,1,0:T(8,128)(2,1)}, u32[]{:S(2)}) copy-start(bf16[4,2,128,128]{3,2,1,0:T(8,128)(2,1)} %param.6) | copy-start | bytes 786436
  7.2 56.1 %all-gather.14.cloned.1.call-start = ((), (), s32[]{:S(2)}) async-start(), calls=%async_computation.10 | async-start | bytes 4456448 | tf_op jit(solution)/shard_map/all_gather | solution.py:42
  7.9 108.6 %all-gather.8.cloned.1.call-start = ((), (), s32[]{:S(2)}) async-start(), calls=%async_computation.5 | async-start | bytes 4456448 | tf_op jit(solution)/shard_map/all_gather | solution.py:42
  8.7 161.1 %all-gather.6.cloned.1.call-start = ((), (), s32[]{:S(2)}) async-start(), calls=%async_computation.4 | async-start | bytes 4456448 | tf_op jit(solution)/shard_map/all_gather | solution.py:42
  9.4 228.1 %reduce-scatter.5.cloned.1.call-start = ((), (), s32[]{:S(2)}) async-start(), calls=%async_computation.6 | async-start | bytes 4718592 | tf_op jit(solution)/shard_map/reduce_scatter | solution.py:43
  201.1 90.7 %all-gather.10.cloned.1.call-start = ((), (), s32[]{:S(2)}) async-start(), calls=%async_computation.7 | async-start | bytes 4456448 | tf_op jit(solution)/shard_map/all_gather | solution.py:42
  239.3 111.1 %reduce-scatter.11.cloned.1.call-start = ((), (), s32[]{:S(2)}) async-start(), calls=%async_computation.12 | async-start | bytes 4718592 | tf_op jit(solution)/shard_map/reduce_scatter | solution.py:43
  296.9 6.2 %copy-start.4 = (bf16[4,2,128,128]{3,2,1,0:T(8,128)(2,1)S(1)}, bf16[4,2,128,128]{3,2,1,0:T(8,128)(2,1)}, u32[]{:S(2)}) copy-start(bf16[4,2,128,128]{3,2,1,0:T(8,128)(2,1)} %param.8) | copy-start | bytes 786436
  303.1 2.2 copy-start.2
  303.1 2.2 copy-start.3
  313.9 36.5 %copy-start.5 = (bf16[4,2,128,128]{3,2,1,0:T(8,128)(2,1)S(1)}, bf16[4,2,128,128]{3,2,1,0:T(8,128)(2,1)}, u32[]{:S(2)}) copy-start(bf16[4,2,128,128]{3,2,1,0:T(8,128)(2,1)} %param.9) | copy-start | bytes 786436
  314.0 90.8 %all-gather.12.cloned.1.call-start = ((), (), s32[]{:S(2)}) async-start(), calls=%async_computation.8 | async-start | bytes 4456448 | tf_op jit(solution)/shard_map/all_gather | solution.py:42
  352.8 136.3 %reduce-scatter.9.cloned.1.call-start = ((), (), s32[]{:S(2)}) async-start(), calls=%async_computation.11 | async-start | bytes 4718592 | tf_op jit(solution)/shard_map/reduce_scatter | solution.py:43
  363.7 125.4 %reduce-scatter.7.cloned.1.call-start = ((), (), s32[]{:S(2)}) async-start(), calls=%async_computation.9 | async-start | bytes 4718592 | tf_op jit(solution)/shard_map/reduce_scatter | solution.py:43
  419.4 71.7 %copy-start.1 = (bf16[4,2,128,128]{3,2,1,0:T(8,128)(2,1)S(1)}, bf16[4,2,128,128]{3,2,1,0:T(8,128)(2,1)}, u32[]{:S(2)}) copy-start(bf16[4,2,128,128]{3,2,1,0:T(8,128)(2,1)} %param.6) | copy-start | bytes 786436
Sparse Core Ops, SparseCore 0:
  10.1 53.0 all-gather.13
  65.4 51.0 all-gather.7
  118.7 51.0 all-gather.5
  201.2 36.2 reduce-scatter.4
  240.0 51.6 all-gather.9
  314.1 36.2 reduce-scatter.10
  353.1 51.6 all-gather.11
  407.2 36.6 reduce-scatter.8
  446.3 37.4 reduce-scatter.6
where the time goes:
time: 503 us; the launch traced here: 499 us
  waiting for transfers between devices  314 us (62%)
  blocking collectives  63.5 us (13%)
  local copies, waits for them, and re-layouts  50.6 us (10%)
  other arithmetic  38.5 us (8%)
  matrix products  16.3 us (3%)
  between operations  15.7 us (3%)
    all_gather x5, waiting for transfers between devices, product(): gathered = lax.all_gather(right_blocks, 'row', axis=0, tiled=True)  239 us
    reduce_scatter x4, waiting for transfers between devices, product(): lax.psum_scatter(partial_blocks(left_blocks, gathered, targets), 'col', s...  72.8 us
    psum x1, blocking collectives, per_device(): lax.psum(local_trace, ('row', 'col'))  63.5 us
    reduce_sum x3, other arithmetic, partial_blocks(): picked = jnp.where(matched[..., None, None], right_rows[:, :, :, None, :,...  29.8 us
    gather x5, local copies, waits for them, and re-layouts, partial_blocks(): right_rows = gathered[safe_rows]  26.1 us
    dot_general x5, matrix products, partial_blocks(): jnp.einsum('iapr,gisaqr->gispq', left_blocks, picked, preferred_element_t...  16.3 us
    transpose x3, local copies, waits for them, and re-layouts, partial_blocks(): jnp.einsum('iapr,gisaqr->gispq', left_blocks, picked, preferred_element_t...  16.2 us
  transfers between devices with their start and end apart: 9, of which 7 were waited for; matrix products, arithmetic and copies ran while one was open for 9% of the time, Pallas kernels for 0%

commit v1 on v0

v1 whole, which is shorter than its diff:
```python
import jax
import jax.numpy as jnp
from jax import lax
from jax.experimental import pallas as pl
from jax.experimental.pallas import tpu as pltpu
from jax.sharding import PartitionSpec as P

MESH = pl.DeviceIdType.MESH
BF = jnp.bfloat16
F32 = jnp.float32
ZERO = 128
TZERO = 16


def kernel(
    cols, step, inter, dens, fock, out, trace,
    r_i, r_d, r_k, l_p, l_s, l_c, parts, landed, own, x_send, x_recv0, x_recv1, t_src, t_buf, pick, tpick,
    p1_send, p1_recv_a, p1_recv_b, p1_local, p2_send, p2_recv_a, p2_recv_b,
    l_send, l_recv, l_local, rs_send, rs_recv, x_ssem, x_rsem, x_local, t_send, t_recv,
):
    row = lax.axis_index("row")
    col = lax.axis_index("col")
    x, k = col // 2, col % 2
    y, z = row // 4, row % 4
    h = z // 2
    zz = z % 2

    x_recv = (x_recv0, x_recv1)

    def dev(x_, k_, y_, z_):
        return (y_ * 4 + z_, x_ * 2 + k_)

    def remote(src, dst, ssem, rsem, target):
        return pltpu.make_async_remote_copy(src, dst, ssem, rsem, device_id=target, device_id_type=MESH)

    barrier = pltpu.get_barrier_semaphore()
    for d in range(1, 8):
        pl.semaphore_signal(barrier, 1, device_id=(row, (col + d) % 8), device_id_type=MESH)
    for d in range(1, 4):
        for kk in range(2):
            pl.semaphore_signal(barrier, 1, device_id=dev(x, kk, (y + d) % 4, z), device_id_type=MESH)
            pl.semaphore_signal(barrier, 1, device_id=dev(x, kk, y, (z + d) % 4), device_id_type=MESH)
    for q in range(2):
        is_self = (x == y) & (k == h) & (zz == q)

        @pl.when(jnp.logical_not(is_self))
        def _():
            pl.semaphore_signal(barrier, 1, device_id=dev(y, h, x, 2 * k + q), device_id_type=MESH)

    r_i[ZERO] = jnp.zeros((128, 128), BF)
    r_d[ZERO] = jnp.zeros((128, 128), BF)
    r_k[ZERO] = jnp.zeros((128, 128), BF)
    x_recv0[TZERO] = jnp.zeros((128, 128), BF)
    x_recv1[TZERO] = jnp.zeros((128, 128), BF)
    pl.semaphore_wait(barrier, 21 - jnp.where((x == y) & (k == h), 1, 0))

    gathers = ((inter, r_i), (dens, r_d), (fock, r_k))

    def p1_copy(m, d):
        tile, buf = gathers[m]
        slot_a = (y * 2 + zz) * 8
        slot_b = (8 + zz * 4 + y) * 8
        kind, off = d
        if kind == "a":
            return remote(tile, buf.at[pl.ds(slot_a, 8)], p1_send.at[m, off], p1_recv_a.at[m, zz], dev(x, h, y, (z + off) % 4))
        return remote(tile, buf.at[pl.ds(slot_b, 8)], p1_send.at[m, off], p1_recv_b.at[m, y], dev(x, h, (y + off) % 4, z))

    def p1_local_copy(m):
        tile, buf = gathers[m]
        slot = jnp.where(k == 0, y * 2 + zz, 8 + zz * 4 + y) * 8
        return pltpu.make_async_copy(tile, buf.at[pl.ds(slot, 8)], p1_local.at[m])

    def p1_start(m):
        for off in (1, 3, 2, 0):
            go = (k != h) if off == 0 else True

            @pl.when((k == 0) & go)
            def _():
                p1_copy(m, ("a", off)).start()

            @pl.when((k == 1) & go)
            def _():
                p1_copy(m, ("b", off)).start()

        @pl.when(k == h)
        def _():
            p1_local_copy(m).start()

    def p1_wait_send(m):
        for off in (1, 3, 2, 0):
            go = (k != h) if off == 0 else True

            @pl.when((k == 0) & go)
            def _():
                p1_copy(m, ("a", off)).wait_send()

            @pl.when((k == 1) & go)
            def _():
                p1_copy(m, ("b", off)).wait_send()

    def recv_wait(buf, start, n, sem):
        view = buf.at[pl.ds(start, n)]
        remote(view, view, sem, sem, dev(x, 1 - k, y, z)).wait_recv()

    def p1_wait(m):
        tile, buf = gathers[m]

        @pl.when(k == h)
        def _():
            p1_local_copy(m).wait()

        for q in range(2):
            mine = (k == 0) & (h == 0) & (zz == q)

            @pl.when(jnp.logical_not(mine))
            def _():
                recv_wait(buf, (y * 2 + q) * 8, 8, p1_recv_a.at[m, q])

        for yy in range(4):
            mine = (k == 1) & (y == yy)

            @pl.when((k == h) & jnp.logical_not(mine))
            def _():
                recv_wait(buf, (8 + zz * 4 + yy) * 8, 8, p1_recv_b.at[m, yy])

    def p2_a(m, off):
        buf = gathers[m][1]
        view = buf.at[pl.ds(y * 16, 16)]
        return remote(view, view, p2_send.at[m, 0, off], p2_recv_a.at[m, y], dev(x, k, (y + off) % 4, z))

    def p2_b(m, off):
        buf = gathers[m][1]
        view = buf.at[pl.ds(64 + zz * 32, 32)]
        return remote(view, view, p2_send.at[m, 1, off], p2_recv_b.at[m, zz], dev(x, k, y, (z + off) % 4))

    def p2_start(m):
        for off in (2, 1, 3):
            p2_a(m, off).start()

            @pl.when(k == h)
            def _():
                p2_b(m, off).start()

    def p2_wait(m):
        buf = gathers[m][1]
        for yy in range(4):
            @pl.when(y != yy)
            def _():
                recv_wait(buf, yy * 16, 16, p2_recv_a.at[m, yy])
        for q in range(2):
            @pl.when(jnp.logical_not((k == h) & (zz == q)))
            def _():
                recv_wait(buf, 64 + q * 32, 32, p2_recv_b.at[m, q])

    def p2_wait_send(m):
        for off in (2, 1, 3):
            p2_a(m, off).wait_send()

            @pl.when(k == h)
            def _():
                p2_b(m, off).wait_send()

    def l_swap(n, src, buf):
        return remote(src, buf.at[k], l_send.at[n], l_recv.at[n], dev(x, 1 - k, y, z))

    l_swap(0, step, l_p).start()
    pltpu.make_async_copy(step, l_p.at[k], l_local.at[0]).start()
    p1_start(0)
    p1_start(1)
    p1_start(2)

    base = row * 4

    def make_pick(n, carry):
        i, t, s = n // 8, (n // 2) % 4, n % 2
        j = cols[base + i, (2 * t + k) * 2 + s]
        jj = jnp.maximum(j, 0)
        w, q = jj & 3, (jj >> 2) & 1
        for a in range(4):
            c = a // 2
            kk = cols[base + i, 4 * x + a]
            tile = t * 2 + q if c == 0 else 8 + q * 4 + t
            block = tile * 8 + w * 2
            live = (j >= 0) & (kk >= 0)
            first = cols[jj, 4 * x + 2 * c]
            second = cols[jj, 4 * x + 2 * c + 1]
            got = jnp.where(first == kk, block, jnp.where(second == kk, block + 1, ZERO))
            pick[n * 4 + a] = jnp.where(live, got, ZERO)
        return carry

    def make_tpick(n, carry):
        i, s = n // 2, n % 2
        j = cols[base + i, col * 2 + s]
        jj = jnp.maximum(j, 0)
        w, q = jj & 3, (jj >> 2) & 1
        block = q * 8 + w * 2
        g = (2 * y + h) * 2
        first = cols[jj, g]
        second = cols[jj, g + 1]
        got = jnp.where(first == base + i, block, jnp.where(second == base + i, block + 1, TZERO))
        tpick[n] = jnp.where(j >= 0, got, TZERO)
        return carry

    lax.fori_loop(0, 32, make_pick, 0)
    lax.fori_loop(0, 8, make_tpick, 0)

    for m in range(3):
        p1_wait(m)
        p2_start(m)

    def rs_copy(n, off):
        return remote(
            parts.at[n, (x + off) % 4], landed.at[n, off], rs_send.at[n, off], rs_recv.at[n, off],
            dev((x + off) % 4, k, y, z),
        )

    def stage(n, left, right):
        for off in (2, 1, 3, 0):
            t = (x + off) % 4

            def one_row(i, carry):
                lhs = jnp.concatenate([left[a // 2, i * 2 + a % 2] for a in range(4)], axis=1)
                rhs = jnp.concatenate(
                    [
                        jnp.concatenate([right[pick[((i * 4 + t) * 2 + s) * 4 + a]] for a in range(4)], axis=1)
                        for s in range(2)
                    ],
                    axis=0,
                )
                got = lax.dot_general(lhs, rhs, (((1,), (1,)), ((), ())), preferred_element_type=F32)
                for s in range(2):
                    block = got[:, s * 128 : (s + 1) * 128]
                    if off == 0:
                        own[n, i * 2 + s] = block
                    else:
                        parts[n, t, i * 2 + s] = block.astype(BF)
                return carry

            lax.fori_loop(0, 4, one_row, 0)
            if off != 0:
                rs_copy(n, off).start()

    def rs_wait(n):
        for off in (1, 3, 2):
            rs_copy(n, off).wait()

    def total(n, b):
        acc = own[n, b]
        for off in (1, 3, 2):
            acc = acc + landed[n, off, b].astype(F32)
        return acc

    def x_copy(n, q):
        return remote(
            x_send.at[n], x_recv[n].at[pl.ds(zz * 8, 8)], x_ssem.at[n, q], x_rsem.at[n, zz],
            dev(y, h, x, 2 * k + q),
        )

    def x_local_copy(n):
        return pltpu.make_async_copy(x_send.at[n], x_recv[n].at[pl.ds(zz * 8, 8)], x_local.at[n])

    def x_self(q):
        return (x == y) & (k == h) & (zz == q)

    def x_start(n):
        for q in range(2):
            @pl.when(jnp.logical_not(x_self(q)))
            def _():
                x_copy(n, q).start()

            @pl.when(x_self(q))
            def _():
                x_local_copy(n).start()

    def x_wait(n):
        for q in range(2):
            @pl.when(jnp.logical_not(x_self(q)))
            def _():
                x_copy(n, q).wait_send()
                recv_wait(x_recv[n], q * 8, 8, x_rsem.at[n, q])

            @pl.when(x_self(q))
            def _():
                x_local_copy(n).wait()

    def flipped(n, b):
        return x_recv[n][tpick[b]].astype(F32).T

    pltpu.make_async_copy(step, l_p.at[k], l_local.at[0]).wait()
    l_swap(0, step, l_p).wait()
    p2_wait(0)
    stage(0, l_p, r_i)
    rs_wait(0)

    def s_block(b, carry):
        l_s[k, b] = total(0, b).astype(BF)
        return carry

    lax.fori_loop(0, 8, s_block, 0)
    l_swap(1, l_s.at[k], l_s).start()
    p2_wait(1)
    l_swap(1, l_s.at[k], l_s).wait()

    stage(1, l_s, r_d)
    rs_wait(1)

    def x_block(b, carry):
        v = total(1, b)
        own[1, b] = v
        x_send[0, b] = v.astype(BF)
        return carry

    lax.fori_loop(0, 8, x_block, 0)
    x_start(0)
    x_wait(0)

    def c_block(b, acc):
        c = (-(own[1, b] + flipped(0, b))).astype(BF)
        l_c[k, b] = c
        prod = c.astype(F32) * fock[b].astype(F32)
        return acc + prod.reshape(16, 8, 128).sum(axis=0)

    tsum = lax.fori_loop(0, 8, c_block, jnp.zeros((8, 128), F32))
    l_swap(2, l_c.at[k], l_c).start()

    def t_copy(level, off):
        if level == 0:
            target, slot = (row, (col + off) % 8), col
        elif level == 1:
            target, slot = dev(x, k, (y + off) % 4, z), y
        else:
            target, slot = dev(x, k, y, (z + off) % 4), z
        return remote(t_src.at[level], t_buf.at[level, slot], t_send.at[level, off], t_recv.at[level, slot], target)

    sizes = (8, 4, 4)
    mine = (col, y, z)

    def t_start(level, value):
        t_src[level] = value
        for off in range(1, sizes[level]):
            t_copy(level, off).start()

    def t_finish(level, value):
        acc = jnp.zeros((8, 128), F32)
        for q in range(sizes[level]):
            @pl.when(mine[level] != q)
            def _():
                remote(
                    t_src.at[level], t_buf.at[level, q], t_recv.at[level, q], t_recv.at[level, q], dev(x, 1 - k, y, z)
                ).wait_recv()

        for off in range(1, sizes[level]):
            t_copy(level, off).wait_send()
        for q in range(sizes[level]):
            acc = acc + jnp.where(mine[level] == q, value, t_buf[level, q])
        return acc

    t_start(0, tsum)
    p2_wait(2)
    l_swap(2, l_c.at[k], l_c).wait()

    stage(2, l_c, r_k)
    tsum = t_finish(0, tsum)
    t_start(1, tsum)
    rs_wait(2)

    def w_block(b, carry):
        v = total(2, b)
        own[2, b] = v
        x_send[1, b] = v.astype(BF)
        return carry

    lax.fori_loop(0, 8, w_block, 0)
    x_start(1)
    tsum = t_finish(1, tsum)
    t_start(2, tsum)
    for m in range(3):
        p1_wait_send(m)
        p2_wait_send(m)
    tsum = t_finish(2, tsum)
    trace[0, 0] = jnp.sum(tsum) * (1.0 / 1048576.0)
    x_wait(1)

    def o_block(b, carry):
        out[b] = (flipped(1, b) - own[2, b]).astype(BF)
        return carry

    lax.fori_loop(0, 8, o_block, 0)


def per_device(block_cols, step_dir, intersection, density, kohn_sham):
    flat = lambda a: a.reshape(8, 128, 128)
    vmem = pl.BlockSpec(memory_space=pltpu.VMEM)
    smem = pl.BlockSpec(memory_space=pltpu.SMEM)
    dma = pltpu.SemaphoreType.DMA
    blk = (128, 128)
    out, trace = pl.pallas_call(
        kernel,
        out_shape=(jax.ShapeDtypeStruct((8, 128, 128), BF), jax.ShapeDtypeStruct((1, 1), F32)),
        in_specs=[smem, vmem, vmem, vmem, vmem],
        out_specs=(vmem, smem),
        scratch_shapes=[
            pltpu.VMEM((129,) + blk, BF), pltpu.VMEM((129,) + blk, BF), pltpu.VMEM((129,) + blk, BF),
            pltpu.VMEM((2, 8) + blk, BF), pltpu.VMEM((2, 8) + blk, BF), pltpu.VMEM((2, 8) + blk, BF),
            pltpu.VMEM((3, 4, 8) + blk, BF), pltpu.VMEM((3, 4, 8) + blk, BF), pltpu.VMEM((3, 8) + blk, F32),
            pltpu.VMEM((2, 8) + blk, BF), pltpu.VMEM((17,) + blk, BF), pltpu.VMEM((17,) + blk, BF),
            pltpu.VMEM((3, 8, 128), F32), pltpu.VMEM((3, 8, 8, 128), F32),
            pltpu.SMEM((128,), jnp.int32), pltpu.SMEM((8,), jnp.int32),
            dma((3, 4)), dma((3, 2)), dma((3, 4)), dma((3,)), dma((3, 2, 4)), dma((3, 4)), dma((3, 2)),
            dma((3,)), dma((3,)), dma((1,)), dma((3, 4)), dma((3, 4)), dma((2, 2)), dma((2, 2)), dma((2,)),
            dma((3, 8)), dma((3, 8)),
        ],
        compiler_params=pltpu.CompilerParams(
            collective_id=0, has_side_effects=True, vmem_limit_bytes=48 * 2**20
        ),
        name="hessian",
    )(block_cols, flat(step_dir), flat(intersection), flat(density), flat(kohn_sham))
    return out.reshape(4, 2, 128, 128), trace.reshape(())


def solution(mesh):
    spec = P("row", "col", None, None)
    return jax.shard_map(
        per_device, mesh=mesh, in_specs=(P(), spec, spec, spec, spec), out_specs=(spec, P()), check_vma=False
    )
```

time: 503 us -> 176 us (0.35)
  waiting for transfers between devices: 314 us -> 0 us
  Pallas kernels: 0 us -> 168 us
  blocking collectives: 63.5 us -> 0 us
  local copies, waits for them, and re-layouts: 50.6 us -> 5.28 us
  other arithmetic: 38.5 us -> 0 us
  matrix products: 16.3 us -> 0 us
  between operations: 15.7 us -> 2.39 us
    all_gather x5 -> x0, waiting for transfers between devices: 239 us -> none  [product(): gathered = lax.all_gather(right_blocks, 'row', axis=0, tiled=True)]
    pallas_call x0 -> x1, Pallas kernels: none -> 168 us  [per_device(): pl.pallas_call(kernel, out_shape=(jax.ShapeDtypeStruct((8, 128, 128), BF)...]
    reduce_scatter x4 -> x0, waiting for transfers between devices: 72.8 us -> none  [product(): lax.psum_scatter(partial_blocks(left_blocks, gathered, targets), 'col', s...]
    psum x1 -> x0, blocking collectives: 63.5 us -> none  [per_device(): lax.psum(local_trace, ('row', 'col'))]
    reduce_sum x4 -> x0, other arithmetic: 32.2 us -> none  [the longest x3 29.8 us: partial_blocks(): picked = jnp.where(matched[..., None, None], right_rows[:, :, :, None, :,...]
    gather x6 -> x0, local copies, waits for them, and re-layouts: 26.7 us -> none  [the longest x5 26.1 us: partial_blocks(): right_rows = gathered[safe_rows]]
    dot_general x5 -> x0, matrix products: 16.3 us -> none  [partial_blocks(): jnp.einsum('iapr,gisaqr->gispq', left_blocks, picked, preferred_element_t...]
    transpose x3 -> x0, local copies, waits for them, and re-layouts: 16.2 us -> none  [partial_blocks(): jnp.einsum('iapr,gisaqr->gispq', left_blocks, picked, preferred_element_t...]
  transfers between devices with their start and end apart: 9 -> 0, of which waited for: 7 -> 0; matrix products, arithmetic and copies ran while one was open for 9% -> 0% of each run, Pallas kernels for 0% -> 0%
where the time goes in v1:
time: 176 us
  Pallas kernels  168 us (95%)
  local copies, waits for them, and re-layouts  5.28 us (3%)
  between operations  2.39 us (1%)
    pallas_call x1, Pallas kernels, per_device(): pl.pallas_call(kernel, out_shape=(jax.ShapeDtypeStruct((8, 128, 128), BF)...  168 us
    unnamed x10, local copies, waits for them, and re-layouts  5.28 us

profile of v1, /device:TPU:39, one launch (start us, length us, event | category | flops | bytes accessed | tf_op | source)
XLA Modules:
  0.0 175.9 jit_solution(13950245206466724717)
XLA Ops:
  0.6 0.8 copy.7.cols
  1.4 0.0 copy-start
  1.4 0.9 copy-done
  2.4 0.0 copy-start.1
  2.4 0.9 copy-done.1
  3.3 0.0 copy-start.2
  3.3 0.9 copy-done.2
  4.3 0.0 copy-start.3
  4.3 0.9 copy-done.3
  5.2 168.2 %hessian.1 = (bf16[8,128,128]{2,1,0:T(8,128)(2,1)S(1)}, f32[1,1]{1,0:T(1,128)}) custom-call(s32[64,16]{1,0:T(8,128)S(1)} %copy.7.cols, bf16[8,128,128]{2,1,0:T(8,128)(2,1)S(1)} %bitcast.7, bf16[8,128,128]{2,1,0:T(8,128)(2,1)S(1)} %bitcast.8, bf16[8,128,128]{2,1,0:T(8,128)(2,1)S(1)} %bitcast.9, bf16[8,128,128]{2,1,0:T(8,128)(2,1)S(1)} %bitcast.10), custom_call_target="tpu_custom_call" | custom-call | tf_op jit(solution)/shard_map/hessian/pallas_call | solution.py:397
  173.4 0.7 copy.10
Async XLA Ops:
  1.4 1.0 copy-start
  2.4 0.9 copy-start.1
  3.3 0.9 copy-start.2
  4.3 0.9 copy-start.3

commit v2 on v1

--- a/solution.py
+++ b/solution.py
@@ -16,7 +16,7 @@
     cols, step, inter, dens, fock, out, trace,
     r_i, r_d, r_k, l_p, l_s, l_c, parts, landed, own, x_send, x_recv0, x_recv1, t_src, t_buf, pick, tpick,
     p1_send, p1_recv_a, p1_recv_b, p1_local, p2_send, p2_recv_a, p2_recv_b,
-    l_send, l_recv, l_local, rs_send, rs_recv, x_ssem, x_rsem, x_local, t_send, t_recv,
+    l_send, l_recv, l_local, rs_send, rs_recv, x_ssem, x_rsem, x_local, relay, rl_ssem, rl_rsem, rl_fsem, t_send, t_recv,
 ):
     row = lax.axis_index("row")
     col = lax.axis_index("col")
@@ -47,12 +47,17 @@
         def _():
             pl.semaphore_signal(barrier, 1, device_id=dev(y, h, x, 2 * k + q), device_id_type=MESH)
 
+    for q in range(2):
+        @pl.when((h == 1) & (x != y))
+        def _():
+            pl.semaphore_signal(barrier, 1, device_id=dev(y, 1, y, 2 * k + q), device_id_type=MESH)
+
     r_i[ZERO] = jnp.zeros((128, 128), BF)
     r_d[ZERO] = jnp.zeros((128, 128), BF)
     r_k[ZERO] = jnp.zeros((128, 128), BF)
     x_recv0[TZERO] = jnp.zeros((128, 128), BF)
     x_recv1[TZERO] = jnp.zeros((128, 128), BF)
-    pl.semaphore_wait(barrier, 21 - jnp.where((x == y) & (k == h), 1, 0))
+    pl.semaphore_wait(barrier, 21 - jnp.where((x == y) & (k == h), 1, 0) + jnp.where((x == y) & (k == 1), 6, 0))
 
     gathers = ((inter, r_i), (dens, r_d), (fock, r_k))
 
@@ -123,42 +128,77 @@
             def _():
                 recv_wait(buf, (8 + zz * 4 + yy) * 8, 8, p1_recv_b.at[m, yy])
 
-    def p2_a(m, off):
+    def p2_a(m, src, half, off, fwd):
         buf = gathers[m][1]
-        view = buf.at[pl.ds(y * 16, 16)]
-        return remote(view, view, p2_send.at[m, 0, off], p2_recv_a.at[m, y], dev(x, k, (y + off) % 4, z))
-
-    def p2_b(m, off):
+        view = buf.at[pl.ds(src * 16 + half * 8, 8)]
+        ssem = p2_send.at[m, 0, fwd * 4 + half * 2 + (off == 3)]
+        return remote(view, view, ssem, p2_recv_a.at[m, src, half], dev(x, k, (y + off) % 4, z))
+
+    def p2_b(m, q, half, off, fwd):
         buf = gathers[m][1]
-        view = buf.at[pl.ds(64 + zz * 32, 32)]
-        return remote(view, view, p2_send.at[m, 1, off], p2_recv_b.at[m, zz], dev(x, k, y, (z + off) % 4))
+        view = buf.at[pl.ds(64 + q * 32 + half * 16, 16)]
+        ssem = p2_send.at[m, 1, fwd * 4 + half * 2 + (off == 3)]
+        return remote(view, view, ssem, p2_recv_b.at[m, q, half], dev(x, k, y, (z + off) % 4))
+
+    ways = ((0, 1), (1, 3), (1, 1), (0, 3))
 
     def p2_start(m):
-        for off in (2, 1, 3):
-            p2_a(m, off).start()
+        for half, off in ways:
+            p2_a(m, y, half, off, 0).start()
 
             @pl.when(k == h)
             def _():
-                p2_b(m, off).start()
+                p2_b(m, zz, half, off, 0).start()
+
+    def p2_wait_a(m, src, half):
+        recv_wait(gathers[m][1], src * 16 + half * 8, 8, p2_recv_a.at[m, src, half])
+
+    def p2_wait_b(m, q, half):
+        recv_wait(gathers[m][1], 64 + q * 32 + half * 16, 16, p2_recv_b.at[m, q, half])
+
+    def near(off):
+        return (z + 4 - off) % 4 // 2 == k
+
+    def p2_relay(m):
+        for half, off in ways[:2]:
+            src = (y + 4 - off) % 4
+            p2_wait_a(m, src, half)
+            p2_a(m, src, half, off, 1).start()
+            q = (z + 4 - off) % 2
+
+            @pl.when(near(off))
+            def _():
+                p2_wait_b(m, q, half)
+                p2_b(m, q, half, off, 1).start()
 
     def p2_wait(m):
-        buf = gathers[m][1]
-        for yy in range(4):
-            @pl.when(y != yy)
-            def _():
-                recv_wait(buf, yy * 16, 16, p2_recv_a.at[m, yy])
-        for q in range(2):
-            @pl.when(jnp.logical_not((k == h) & (zz == q)))
-            def _():
-                recv_wait(buf, 64 + q * 32, 32, p2_recv_b.at[m, q])
+        for half, off in ways[2:]:
+            p2_wait_a(m, (y + 4 - off) % 4, half)
+            q = (z + 4 - off) % 2
+
+            @pl.when(near(off))
+            def _():
+                p2_wait_b(m, q, half)
+        for half in range(2):
+            p2_wait_a(m, (y + 2) % 4, half)
+
+            @pl.when(near(2))
+            def _():
+                p2_wait_b(m, zz, half)
 
     def p2_wait_send(m):
-        for off in (2, 1, 3):
-            p2_a(m, off).wait_send()
+        for half, off in ways:
+            p2_a(m, y, half, off, 0).wait_send()
 
             @pl.when(k == h)
             def _():
-                p2_b(m, off).wait_send()
+                p2_b(m, zz, half, off, 0).wait_send()
+        for half, off in ways[:2]:
+            p2_a(m, (y + 4 - off) % 4, half, off, 1).wait_send()
+
+            @pl.when(near(off))
+            def _():
+                p2_b(m, (z + 4 - off) % 2, half, off, 1).wait_send()
 
     def l_swap(n, src, buf):
         return remote(src, buf.at[k], l_send.at[n], l_recv.at[n], dev(x, 1 - k, y, z))
@@ -166,8 +206,6 @@
     l_swap(0, step, l_p).start()
     pltpu.make_async_copy(step, l_p.at[k], l_local.at[0]).start()
     p1_start(0)
-    p1_start(1)
-    p1_start(2)
 
     base = row * 4
 
@@ -204,9 +242,10 @@
     lax.fori_loop(0, 32, make_pick, 0)
     lax.fori_loop(0, 8, make_tpick, 0)
 
-    for m in range(3):
-        p1_wait(m)
-        p2_start(m)
+    p1_wait(0)
+    p2_start(0)
+    p1_start(1)
+    p2_relay(0)
 
     def rs_copy(n, off):
         return remote(
@@ -262,26 +301,72 @@
     def x_self(q):
         return (x == y) & (k == h) & (zz == q)
 
+    def to_relay(n, c):
+        return remote(
+            x_send.at[n, pl.ds(c * 4, 4)], relay.at[n, y, pl.ds(c * 4, 4)], rl_ssem.at[n, c], rl_rsem.at[n, y, c],
+            dev(x, k, x, z),
+        )
+
+    def from_relay(n, yy, c, q):
+        return remote(
+            relay.at[n, yy, pl.ds(c * 4, 4)], x_recv[n].at[pl.ds(zz * 8 + c * 4, 4)], rl_fsem.at[n, yy, c * 2 + q],
+            x_rsem.at[n, zz], dev(yy, h, x, 2 * k + q),
+        )
+
+    by_relay = (k == 1) & (x != y)
+    is_relay = (k == 1) & (x == y)
+
     def x_start(n):
+        @pl.when(by_relay)
+        def _():
+            for c in range(2):
+                to_relay(n, c).start()
+
         for q in range(2):
-            @pl.when(jnp.logical_not(x_self(q)))
+            @pl.when(jnp.logical_not(x_self(q) | by_relay))
             def _():
                 x_copy(n, q).start()
 
             @pl.when(x_self(q))
             def _():
                 x_local_copy(n).start()
+
+    def x_relay(n):
+        @pl.when(is_relay)
+        def _():
+            for c in range(2):
+                for o in (1, 3, 2):
+                    yy = (y + o) % 4
+                    view = relay.at[n, yy, pl.ds(c * 4, 4)]
+                    remote(view, view, rl_ssem.at[n, c], rl_rsem.at[n, yy, c], dev(x, 1 - k, y, z)).wait_recv()
+                    for q in range(2):
+                        from_relay(n, yy, c, q).start()
 
     def x_wait(n):
         for q in range(2):
             @pl.when(jnp.logical_not(x_self(q)))
             def _():
+                recv_wait(x_recv[n], q * 8, 8, x_rsem.at[n, q])
+
+            @pl.when(jnp.logical_not(x_self(q) | by_relay))
+            def _():
                 x_copy(n, q).wait_send()
-                recv_wait(x_recv[n], q * 8, 8, x_rsem.at[n, q])
 
             @pl.when(x_self(q))
             def _():
                 x_local_copy(n).wait()
+
+        @pl.when(by_relay)
+        def _():
+            for c in range(2):
+                to_relay(n, c).wait_send()
+
+        @pl.when(is_relay)
+        def _():
+            for c in range(2):
+                for o in (1, 3, 2):
+                    for q in range(2):
+                        from_relay(n, (y + o) % 4, c, q).wait_send()
 
     def flipped(n, b):
         return x_recv[n][tpick[b]].astype(F32).T
@@ -290,6 +375,9 @@
     l_swap(0, step, l_p).wait()
     p2_wait(0)
     stage(0, l_p, r_i)
+    p1_wait(1)
+    p2_start(1)
+    p1_start(2)
     rs_wait(0)
 
     def s_block(b, carry):
@@ -298,10 +386,13 @@
 
     lax.fori_loop(0, 8, s_block, 0)
     l_swap(1, l_s.at[k], l_s).start()
+    p2_relay(1)
     p2_wait(1)
     l_swap(1, l_s.at[k], l_s).wait()
 
     stage(1, l_s, r_d)
+    p1_wait(2)
+    p2_start(2)
     rs_wait(1)
 
     def x_block(b, carry):
@@ -312,6 +403,8 @@
 
     lax.fori_loop(0, 8, x_block, 0)
     x_start(0)
+    x_relay(0)
+    p2_relay(2)
     x_wait(0)
 
     def c_block(b, acc):
@@ -372,6 +465,7 @@
 
     lax.fori_loop(0, 8, w_block, 0)
     x_start(1)
+    x_relay(1)
     tsum = t_finish(1, tsum)
     t_start(2, tsum)
     for m in range(3):
@@ -406,8 +500,9 @@
             pltpu.VMEM((2, 8) + blk, BF), pltpu.VMEM((17,) + blk, BF), pltpu.VMEM((17,) + blk, BF),
             pltpu.VMEM((3, 8, 128), F32), pltpu.VMEM((3, 8, 8, 128), F32),
             pltpu.SMEM((128,), jnp.int32), pltpu.SMEM((8,), jnp.int32),
-            dma((3, 4)), dma((3, 2)), dma((3, 4)), dma((3,)), dma((3, 2, 4)), dma((3, 4)), dma((3, 2)),
+            dma((3, 4)), dma((3, 2)), dma((3, 4)), dma((3,)), dma((3, 2, 8)), dma((3, 4, 2)), dma((3, 2, 2)),
             dma((3,)), dma((3,)), dma((1,)), dma((3, 4)), dma((3, 4)), dma((2, 2)), dma((2, 2)), dma((2,)),
+            pltpu.VMEM((2, 4, 8) + blk, BF), dma((2, 2)), dma((2, 4, 2)), dma((2, 4, 4)),
             dma((3, 8)), dma((3, 8)),
         ],
         compiler_params=pltpu.CompilerParams(

time: 176 us -> 150 us (0.85)
  Pallas kernels: 168 us -> 142 us
    pallas_call x1, Pallas kernels: 168 us -> 142 us  [per_device(): pl.pallas_call(kernel, out_shape=(jax.ShapeDtypeStruct((8, 128, 128), BF)...]
where the time goes in v2:
time: 150 us
  Pallas kernels  142 us (95%)
  local copies, waits for them, and re-layouts  5.28 us (4%)
  between operations  2.39 us (2%)
    pallas_call x1, Pallas kernels, per_device(): pl.pallas_call(kernel, out_shape=(jax.ShapeDtypeStruct((8, 128, 128), BF)...  142 us
    unnamed x10, local copies, waits for them, and re-layouts  5.28 us

profile of v2, /device:TPU:39, one launch (start us, length us, event | category | flops | bytes accessed | tf_op | source)
XLA Modules:
  0.0 149.7 jit_solution(7016167096080075695)
XLA Ops:
  0.6 0.8 copy.7.cols
  1.4 0.0 copy-start
  1.4 0.9 copy-done
  2.4 0.0 copy-start.1
  2.4 0.9 copy-done.1
  3.3 0.0 copy-start.2
  3.3 0.9 copy-done.2
  4.3 0.0 copy-start.3
  4.3 0.9 copy-done.3
  5.2 142.0 %hessian.1 = (bf16[8,128,128]{2,1,0:T(8,128)(2,1)S(1)}, f32[1,1]{1,0:T(1,128)}) custom-call(s32[64,16]{1,0:T(8,128)S(1)} %copy.7.cols, bf16[8,128,128]{2,1,0:T(8,128)(2,1)S(1)} %bitcast.7, bf16[8,128,128]{2,1,0:T(8,128)(2,1)S(1)} %bitcast.8, bf16[8,128,128]{2,1,0:T(8,128)(2,1)S(1)} %bitcast.9, bf16[8,128,128]{2,1,0:T(8,128)(2,1)S(1)} %bitcast.10), custom_call_target="tpu_custom_call" | custom-call | tf_op jit(solution)/shard_map/hessian/pallas_call | solution.py:491
  147.2 0.7 copy.10
Async XLA Ops:
  1.4 1.0 copy-start
  2.4 0.9 copy-start.1
  3.3 0.9 copy-start.2
  4.3 0.9 copy-start.3

commit v3 on v2

--- a/solution.py
+++ b/solution.py
@@ -13,11 +13,16 @@
 
 
 def kernel(
-    cols, step, inter, dens, fock, out, trace,
+    cols_hbm, step, inter, dens, fock_hbm, out, trace,
+    cols, fock, in_sem,
     r_i, r_d, r_k, l_p, l_s, l_c, parts, landed, own, x_send, x_recv0, x_recv1, t_src, t_buf, pick, tpick,
     p1_send, p1_recv_a, p1_recv_b, p1_local, p2_send, p2_recv_a, p2_recv_b,
     l_send, l_recv, l_local, rs_send, rs_recv, x_ssem, x_rsem, x_local, relay, rl_ssem, rl_rsem, rl_fsem, t_send, t_recv,
 ):
+    cols_copy = pltpu.make_async_copy(cols_hbm, cols, in_sem.at[0])
+    cols_copy.start()
+    fock_copy = pltpu.make_async_copy(fock_hbm, fock, in_sem.at[1])
+    fock_copy.start()
     row = lax.axis_index("row")
     col = lax.axis_index("col")
     x, k = col // 2, col % 2
@@ -59,7 +64,7 @@
     x_recv1[TZERO] = jnp.zeros((128, 128), BF)
     pl.semaphore_wait(barrier, 21 - jnp.where((x == y) & (k == h), 1, 0) + jnp.where((x == y) & (k == 1), 6, 0))
 
-    gathers = ((inter, r_i), (dens, r_d), (fock, r_k))
+    gathers = ((inter, r_i), (dens, r_d), (fock_hbm, r_k))
 
     def p1_copy(m, d):
         tile, buf = gathers[m]
@@ -200,12 +205,19 @@
             def _():
                 p2_b(m, (z + 4 - off) % 2, half, off, 1).wait_send()
 
-    def l_swap(n, src, buf):
-        return remote(src, buf.at[k], l_send.at[n], l_recv.at[n], dev(x, 1 - k, y, z))
-
-    l_swap(0, step, l_p).start()
+    def l_swap(n, src, buf, c):
+        part = pl.ds(c * 4, 4)
+        return remote(src.at[part], buf.at[k, part], l_send.at[n, c], l_recv.at[n, c], dev(x, 1 - k, y, z))
+
+    def l_wait(n, src, buf):
+        for c in range(2):
+            l_swap(n, src, buf, c).wait()
+
     pltpu.make_async_copy(step, l_p.at[k], l_local.at[0]).start()
     p1_start(0)
+    for c in range(2):
+        l_swap(0, step, l_p, c).start()
+    p1_start(1)
 
     base = row * 4
 
@@ -239,22 +251,26 @@
         tpick[n] = jnp.where(j >= 0, got, TZERO)
         return carry
 
+    cols_copy.wait()
+    fock_copy.wait()
     lax.fori_loop(0, 32, make_pick, 0)
     lax.fori_loop(0, 8, make_tpick, 0)
 
     p1_wait(0)
     p2_start(0)
-    p1_start(1)
     p2_relay(0)
-
-    def rs_copy(n, off):
+    p1_wait(1)
+    p2_start(1)
+
+    def rs_copy(n, off, c):
+        part = pl.ds(c * 4, 4)
         return remote(
-            parts.at[n, (x + off) % 4], landed.at[n, off], rs_send.at[n, off], rs_recv.at[n, off],
+            parts.at[n, (x + off) % 4, part], landed.at[n, off, part], rs_send.at[n, off, c], rs_recv.at[n, off, c],
             dev((x + off) % 4, k, y, z),
         )
 
     def stage(n, left, right):
-        for off in (2, 1, 3, 0):
+        def rows(off, lo, hi):
             t = (x + off) % 4
 
             def one_row(i, carry):
@@ -275,13 +291,17 @@
                         parts[n, t, i * 2 + s] = block.astype(BF)
                 return carry
 
-            lax.fori_loop(0, 4, one_row, 0)
-            if off != 0:
-                rs_copy(n, off).start()
-
-    def rs_wait(n):
+            lax.fori_loop(lo, hi, one_row, 0)
+
+        for c in range(2):
+            for off in (2, 1, 3):
+                rows(off, c * 2, c * 2 + 2)
+                rs_copy(n, off, c).start()
+        rows(0, 0, 4)
+
+    def rs_wait(n, c):
         for off in (1, 3, 2):
-            rs_copy(n, off).wait()
+            rs_copy(n, off, c).wait()
 
     def total(n, b):
         acc = own[n, b]
@@ -289,14 +309,16 @@
             acc = acc + landed[n, off, b].astype(F32)
         return acc
 
-    def x_copy(n, q):
+    def x_copy(n, q, c):
         return remote(
-            x_send.at[n], x_recv[n].at[pl.ds(zz * 8, 8)], x_ssem.at[n, q], x_rsem.at[n, zz],
-            dev(y, h, x, 2 * k + q),
+            x_send.at[n, pl.ds(c * 4, 4)], x_recv[n].at[pl.ds(zz * 8 + c * 4, 4)], x_ssem.at[n, q, c],
+            x_rsem.at[n, zz], dev(y, h, x, 2 * k + q),
         )
 
-    def x_local_copy(n):
-        return pltpu.make_async_copy(x_send.at[n], x_recv[n].at[pl.ds(zz * 8, 8)], x_local.at[n])
+    def x_local_copy(n, c):
+        return pltpu.make_async_copy(
+            x_send.at[n, pl.ds(c * 4, 4)], x_recv[n].at[pl.ds(zz * 8 + c * 4, 4)], x_local.at[n, c]
+        )
 
     def x_self(q):
         return (x == y) & (k == h) & (zz == q)
@@ -316,31 +338,29 @@
     by_relay = (k == 1) & (x != y)
     is_relay = (k == 1) & (x == y)
 
-    def x_start(n):
+    def x_start(n, c):
         @pl.when(by_relay)
         def _():
-            for c in range(2):
-                to_relay(n, c).start()
+            to_relay(n, c).start()
 
         for q in range(2):
             @pl.when(jnp.logical_not(x_self(q) | by_relay))
             def _():
-                x_copy(n, q).start()
+                x_copy(n, q, c).start()
 
             @pl.when(x_self(q))
             def _():
-                x_local_copy(n).start()
-
-    def x_relay(n):
+                x_local_copy(n, c).start()
+
+    def x_relay(n, c):
         @pl.when(is_relay)
         def _():
-            for c in range(2):
-                for o in (1, 3, 2):
-                    yy = (y + o) % 4
-                    view = relay.at[n, yy, pl.ds(c * 4, 4)]
-                    remote(view, view, rl_ssem.at[n, c], rl_rsem.at[n, yy, c], dev(x, 1 - k, y, z)).wait_recv()
-                    for q in range(2):
-                        from_relay(n, yy, c, q).start()
+            for o in (1, 3, 2):
+                yy = (y + o) % 4
+                view = relay.at[n, yy, pl.ds(c * 4, 4)]
+                remote(view, view, rl_ssem.at[n, c], rl_rsem.at[n, yy, c], dev(x, 1 - k, y, z)).wait_recv()
+                for q in range(2):
+                    from_relay(n, yy, c, q).start()
 
     def x_wait(n):
         for q in range(2):
@@ -348,22 +368,24 @@
             def _():
                 recv_wait(x_recv[n], q * 8, 8, x_rsem.at[n, q])
 
-            @pl.when(jnp.logical_not(x_self(q) | by_relay))
-            def _():
-                x_copy(n, q).wait_send()
-
             @pl.when(x_self(q))
             def _():
-                x_local_copy(n).wait()
-
-        @pl.when(by_relay)
-        def _():
-            for c in range(2):
+                for c in range(2):
+                    x_local_copy(n, c).wait()
+
+    def x_wait_send(n):
+        for c in range(2):
+            for q in range(2):
+                @pl.when(jnp.logical_not(x_self(q) | by_relay))
+                def _():
+                    x_copy(n, q, c).wait_send()
+
+            @pl.when(by_relay)
+            def _():
                 to_relay(n, c).wait_send()
 
-        @pl.when(is_relay)
-        def _():
-            for c in range(2):
+            @pl.when(is_relay)
+            def _():
                 for o in (1, 3, 2):
                     for q in range(2):
                         from_relay(n, (y + o) % 4, c, q).wait_send()
@@ -372,28 +394,25 @@
         return x_recv[n][tpick[b]].astype(F32).T
 
     pltpu.make_async_copy(step, l_p.at[k], l_local.at[0]).wait()
-    l_swap(0, step, l_p).wait()
+    l_wait(0, step, l_p)
     p2_wait(0)
     stage(0, l_p, r_i)
-    p1_wait(1)
-    p2_start(1)
-    p1_start(2)
-    rs_wait(0)
 
     def s_block(b, carry):
         l_s[k, b] = total(0, b).astype(BF)
         return carry
 
-    lax.fori_loop(0, 8, s_block, 0)
-    l_swap(1, l_s.at[k], l_s).start()
-    p2_relay(1)
+    for c in range(2):
+        rs_wait(0, c)
+        lax.fori_loop(c * 4, c * 4 + 4, s_block, 0)
+        l_swap(1, l_s.at[k], l_s, c).start()
+        if c == 0:
+            p2_relay(1)
+            p1_start(2)
+    l_wait(1, l_s.at[k], l_s)
     p2_wait(1)
-    l_swap(1, l_s.at[k], l_s).wait()
 
     stage(1, l_s, r_d)
-    p1_wait(2)
-    p2_start(2)
-    rs_wait(1)
 
     def x_block(b, carry):
         v = total(1, b)
@@ -401,9 +420,15 @@
         x_send[0, b] = v.astype(BF)
         return carry
 
-    lax.fori_loop(0, 8, x_block, 0)
-    x_start(0)
-    x_relay(0)
+    for c in range(2):
+        rs_wait(1, c)
+        lax.fori_loop(c * 4, c * 4 + 4, x_block, 0)
+        x_start(0, c)
+        if c == 0:
+            p1_wait(2)
+            p2_start(2)
+    x_relay(0, 0)
+    x_relay(0, 1)
     p2_relay(2)
     x_wait(0)
 
@@ -413,8 +438,10 @@
         prod = c.astype(F32) * fock[b].astype(F32)
         return acc + prod.reshape(16, 8, 128).sum(axis=0)
 
-    tsum = lax.fori_loop(0, 8, c_block, jnp.zeros((8, 128), F32))
-    l_swap(2, l_c.at[k], l_c).start()
+    tsum = jnp.zeros((8, 128), F32)
+    for c in range(2):
+        tsum = lax.fori_loop(c * 4, c * 4 + 4, c_block, tsum)
+        l_swap(2, l_c.at[k], l_c, c).start()
 
     def t_copy(level, off):
         if level == 0:
@@ -450,12 +477,11 @@
 
     t_start(0, tsum)
     p2_wait(2)
-    l_swap(2, l_c.at[k], l_c).wait()
+    l_wait(2, l_c.at[k], l_c)
 
     stage(2, l_c, r_k)
     tsum = t_finish(0, tsum)
     t_start(1, tsum)
-    rs_wait(2)
 
     def w_block(b, carry):
         v = total(2, b)
@@ -463,9 +489,12 @@
         x_send[1, b] = v.astype(BF)
         return carry
 
-    lax.fori_loop(0, 8, w_block, 0)
-    x_start(1)
-    x_relay(1)
+    for c in range(2):
+        rs_wait(2, c)
+        lax.fori_loop(c * 4, c * 4 + 4, w_block, 0)
+        x_start(1, c)
+    x_relay(1, 0)
+    x_relay(1, 1)
     tsum = t_finish(1, tsum)
     t_start(2, tsum)
     for m in range(3):
@@ -474,6 +503,8 @@
     tsum = t_finish(2, tsum)
     trace[0, 0] = jnp.sum(tsum) * (1.0 / 1048576.0)
     x_wait(1)
+    x_wait_send(0)
+    x_wait_send(1)
 
     def o_block(b, carry):
         out[b] = (flipped(1, b) - own[2, b]).astype(BF)
@@ -486,14 +517,16 @@
     flat = lambda a: a.reshape(8, 128, 128)
     vmem = pl.BlockSpec(memory_space=pltpu.VMEM)
     smem = pl.BlockSpec(memory_space=pltpu.SMEM)
+    hbm = pl.BlockSpec(memory_space=pl.ANY)
     dma = pltpu.SemaphoreType.DMA
     blk = (128, 128)
     out, trace = pl.pallas_call(
         kernel,
         out_shape=(jax.ShapeDtypeStruct((8, 128, 128), BF), jax.ShapeDtypeStruct((1, 1), F32)),
-        in_specs=[smem, vmem, vmem, vmem, vmem],
+        in_specs=[hbm] * 5,
         out_specs=(vmem, smem),
         scratch_shapes=[
+            pltpu.SMEM((64, 16), jnp.int32), pltpu.VMEM((8,) + blk, BF), dma((2,)),
             pltpu.VMEM((129,) + blk, BF), pltpu.VMEM((129,) + blk, BF), pltpu.VMEM((129,) + blk, BF),
             pltpu.VMEM((2, 8) + blk, BF), pltpu.VMEM((2, 8) + blk, BF), pltpu.VMEM((2, 8) + blk, BF),
             pltpu.VMEM((3, 4, 8) + blk, BF), pltpu.VMEM((3, 4, 8) + blk, BF), pltpu.VMEM((3, 8) + blk, F32),
@@ -501,12 +534,12 @@
             pltpu.VMEM((3, 8, 128), F32), pltpu.VMEM((3, 8, 8, 128), F32),
             pltpu.SMEM((128,), jnp.int32), pltpu.SMEM((8,), jnp.int32),
             dma((3, 4)), dma((3, 2)), dma((3, 4)), dma((3,)), dma((3, 2, 8)), dma((3, 4, 2)), dma((3, 2, 2)),
-            dma((3,)), dma((3,)), dma((1,)), dma((3, 4)), dma((3, 4)), dma((2, 2)), dma((2, 2)), dma((2,)),
+            dma((3, 2)), dma((3, 2)), dma((1,)), dma((3, 4, 2)), dma((3, 4, 2)), dma((2, 2, 2)), dma((2, 2)), dma((2, 2)),
             pltpu.VMEM((2, 4, 8) + blk, BF), dma((2, 2)), dma((2, 4, 2)), dma((2, 4, 4)),
             dma((3, 8)), dma((3, 8)),
         ],
         compiler_params=pltpu.CompilerParams(
-            collective_id=0, has_side_effects=True, vmem_limit_bytes=48 * 2**20
+            collective_id=0, has_side_effects=True, vmem_limit_bytes=63_900_000
         ),
         name="hessian",
     )(block_cols, flat(step_dir), flat(intersection), flat(density), flat(kohn_sham))

time: 150 us -> 133 us (0.89)
  Pallas kernels: 142 us -> 128 us
  local copies, waits for them, and re-layouts: 5.28 us -> 3.07 us
    pallas_call x1, Pallas kernels: 142 us -> 128 us  [per_device(): pl.pallas_call(kernel, out_shape=(jax.ShapeDtypeStruct((8, 128, 128), BF)...]
    unnamed x10 -> x2, local copies, waits for them, and re-layouts: 5.28 us -> 3.07 us
where the time goes in v3:
time: 133 us
  Pallas kernels  128 us (96%)
  local copies, waits for them, and re-layouts  3.07 us (2%)
  between operations  2.4 us (2%)
    pallas_call x1, Pallas kernels, per_device(): pl.pallas_call(kernel, out_shape=(jax.ShapeDtypeStruct((8, 128, 128), BF)...  128 us
    unnamed x2, local copies, waits for them, and re-layouts  3.07 us

profile of v3, /device:TPU:39, one launch (start us, length us, event | category | flops | bytes accessed | tf_op | source)
XLA Modules:
  0.0 133.1 jit_solution(15938561933280423286)
XLA Ops:
  0.6 1.4 %copy.7.cols_hbm = s32[64,16]{1,0:T(8,128)} copy(s32[64,16]{0,1:T(8,128)} %param.5) | data formatting | bytes 8192 | tf_op args[0]
  2.0 127.6 %hessian.1 = (bf16[8,128,128]{2,1,0:T(8,128)(2,1)}, f32[1,1]{1,0:T(1,128)}) custom-call(s32[64,16]{1,0:T(8,128)} %copy.7.cols_hbm, bf16[8,128,128]{2,1,0:T(8,128)(2,1)} %bitcast.7, bf16[8,128,128]{2,1,0:T(8,128)(2,1)} %bitcast.8, bf16[8,128,128]{2,1,0:T(8,128)(2,1)} %bitcast.9, bf16[8,128,128]{2,1,0:T(8,128)(2,1)} %bitcast.10), custom_call_target="tpu_custom_call" | custom-call | tf_op jit(solution)/shard_map/hessian/pallas_call | solution.py:523
  129.7 1.7 %copy.10 = bf16[4,2,128,128]{3,2,1,0:T(8,128)(2,1)} copy(bf16[4,2,128,128]{3,2,1,0:T(8,128)(2,1)} %bitcast.6) | data formatting | bytes 524288

commit v4 on v3

--- a/solution.py
+++ b/solution.py
@@ -223,30 +223,30 @@
 
     def make_pick(n, carry):
         i, t, s = n // 8, (n // 2) % 4, n % 2
-        j = cols[base + i, (2 * t + k) * 2 + s]
+        j = cols[(2 * t + k) * 2 + s, base + i]
         jj = jnp.maximum(j, 0)
         w, q = jj & 3, (jj >> 2) & 1
         for a in range(4):
             c = a // 2
-            kk = cols[base + i, 4 * x + a]
+            kk = cols[4 * x + a, base + i]
             tile = t * 2 + q if c == 0 else 8 + q * 4 + t
             block = tile * 8 + w * 2
             live = (j >= 0) & (kk >= 0)
-            first = cols[jj, 4 * x + 2 * c]
-            second = cols[jj, 4 * x + 2 * c + 1]
+            first = cols[4 * x + 2 * c, jj]
+            second = cols[4 * x + 2 * c + 1, jj]
             got = jnp.where(first == kk, block, jnp.where(second == kk, block + 1, ZERO))
             pick[n * 4 + a] = jnp.where(live, got, ZERO)
         return carry
 
     def make_tpick(n, carry):
         i, s = n // 2, n % 2
-        j = cols[base + i, col * 2 + s]
+        j = cols[col * 2 + s, base + i]
         jj = jnp.maximum(j, 0)
         w, q = jj & 3, (jj >> 2) & 1
         block = q * 8 + w * 2
         g = (2 * y + h) * 2
-        first = cols[jj, g]
-        second = cols[jj, g + 1]
+        first = cols[g, jj]
+        second = cols[g + 1, jj]
         got = jnp.where(first == base + i, block, jnp.where(second == base + i, block + 1, TZERO))
         tpick[n] = jnp.where(j >= 0, got, TZERO)
         return carry
@@ -522,11 +522,11 @@
     blk = (128, 128)
     out, trace = pl.pallas_call(
         kernel,
-        out_shape=(jax.ShapeDtypeStruct((8, 128, 128), BF), jax.ShapeDtypeStruct((1, 1), F32)),
+        out_shape=(pltpu.VMEM((8, 128, 128), BF), jax.ShapeDtypeStruct((1, 1), F32)),
         in_specs=[hbm] * 5,
         out_specs=(vmem, smem),
         scratch_shapes=[
-            pltpu.SMEM((64, 16), jnp.int32), pltpu.VMEM((8,) + blk, BF), dma((2,)),
+            pltpu.SMEM((16, 64), jnp.int32), pltpu.VMEM((8,) + blk, BF), dma((2,)),
             pltpu.VMEM((129,) + blk, BF), pltpu.VMEM((129,) + blk, BF), pltpu.VMEM((129,) + blk, BF),
             pltpu.VMEM((2, 8) + blk, BF), pltpu.VMEM((2, 8) + blk, BF), pltpu.VMEM((2, 8) + blk, BF),
             pltpu.VMEM((3, 4, 8) + blk, BF), pltpu.VMEM((3, 4, 8) + blk, BF), pltpu.VMEM((3, 8) + blk, F32),
@@ -542,7 +542,7 @@
             collective_id=0, has_side_effects=True, vmem_limit_bytes=63_900_000
         ),
         name="hessian",
-    )(block_cols, flat(step_dir), flat(intersection), flat(density), flat(kohn_sham))
+    )(block_cols.T, flat(step_dir), flat(intersection), flat(density), flat(kohn_sham))
     return out.reshape(4, 2, 128, 128), trace.reshape(())
 
 

time: 133 us -> 131 us (0.985)
  local copies, waits for them, and re-layouts: 3.07 us -> 0.71 us
    unnamed x2 -> x1, local copies, waits for them, and re-layouts: 3.07 us -> 0.71 us
where the time goes in v4:
time: 131 us
  Pallas kernels  128 us (98%)
  between operations  2.33 us (2%)
    pallas_call x1, Pallas kernels, per_device(): pl.pallas_call(kernel, out_shape=(pltpu.VMEM((8, 128, 128), BF), jax.Shap...  128 us

profile of v4, /device:TPU:39, one launch (start us, length us, event | category | flops | bytes accessed | tf_op | source)
XLA Modules:
  0.0 130.6 jit_solution(5122343771820213446)
XLA Ops:
  0.6 127.6 %hessian.1 = (bf16[8,128,128]{2,1,0:T(8,128)(2,1)S(1)}, f32[1,1]{1,0:T(1,128)}) custom-call(s32[16,64]{1,0:T(8,128)} %bitcast.12, bf16[8,128,128]{2,1,0:T(8,128)(2,1)} %bitcast.8, bf16[8,128,128]{2,1,0:T(8,128)(2,1)} %bitcast.9, bf16[8,128,128]{2,1,0:T(8,128)(2,1)} %bitcast.10, bf16[8,128,128]{2,1,0:T(8,128)(2,1)} %bitcast.11), custom_call_target="tpu_custom_call" | custom-call | tf_op jit(solution)/shard_map/hessian/pallas_call | solution.py:523
  128.2 0.7 copy.9

commit v5 on v4

--- a/solution.py
+++ b/solution.py
@@ -46,13 +46,6 @@
             pl.semaphore_signal(barrier, 1, device_id=dev(x, kk, (y + d) % 4, z), device_id_type=MESH)
             pl.semaphore_signal(barrier, 1, device_id=dev(x, kk, y, (z + d) % 4), device_id_type=MESH)
     for q in range(2):
-        is_self = (x == y) & (k == h) & (zz == q)
-
-        @pl.when(jnp.logical_not(is_self))
-        def _():
-            pl.semaphore_signal(barrier, 1, device_id=dev(y, h, x, 2 * k + q), device_id_type=MESH)
-
-    for q in range(2):
         @pl.when((h == 1) & (x != y))
         def _():
             pl.semaphore_signal(barrier, 1, device_id=dev(y, 1, y, 2 * k + q), device_id_type=MESH)
@@ -62,7 +55,7 @@
     r_k[ZERO] = jnp.zeros((128, 128), BF)
     x_recv0[TZERO] = jnp.zeros((128, 128), BF)
     x_recv1[TZERO] = jnp.zeros((128, 128), BF)
-    pl.semaphore_wait(barrier, 21 - jnp.where((x == y) & (k == h), 1, 0) + jnp.where((x == y) & (k == 1), 6, 0))
+    pl.semaphore_wait(barrier, 19 + jnp.where((x == y) & (k == 1), 6, 0))
 
     gathers = ((inter, r_i), (dens, r_d), (fock_hbm, r_k))
 
@@ -424,10 +417,11 @@
         rs_wait(1, c)
         lax.fori_loop(c * 4, c * 4 + 4, x_block, 0)
         x_start(0, c)
+        if c == 1:
+            x_relay(0, 0)
         if c == 0:
             p1_wait(2)
             p2_start(2)
-    x_relay(0, 0)
     x_relay(0, 1)
     p2_relay(2)
     x_wait(0)
@@ -493,10 +487,12 @@
         rs_wait(2, c)
         lax.fori_loop(c * 4, c * 4 + 4, w_block, 0)
         x_start(1, c)
-    x_relay(1, 0)
+        if c == 0:
+            tsum = t_finish(1, tsum)
+            t_start(2, tsum)
+        if c == 1:
+            x_relay(1, 0)
     x_relay(1, 1)
-    tsum = t_finish(1, tsum)
-    t_start(2, tsum)
     for m in range(3):
         p1_wait_send(m)
         p2_wait_send(m)

time: 131 us -> 130 us (level)
  no operation moved by 1% of the time
where the time goes in v5:
time: 130 us
  Pallas kernels  127 us (98%)
  between operations  2.33 us (2%)
    pallas_call x1, Pallas kernels, per_device(): pl.pallas_call(kernel, out_shape=(pltpu.VMEM((8, 128, 128), BF), jax.Shap...  127 us

profile of v5, /device:TPU:39, one launch (start us, length us, event | category | flops | bytes accessed | tf_op | source)
XLA Modules:
  0.0 130.0 jit_solution(15341026481524371119)
XLA Ops:
  0.6 127.0 %hessian.1 = (bf16[8,128,128]{2,1,0:T(8,128)(2,1)S(1)}, f32[1,1]{1,0:T(1,128)}) custom-call(s32[16,64]{1,0:T(8,128)} %bitcast.12, bf16[8,128,128]{2,1,0:T(8,128)(2,1)} %bitcast.8, bf16[8,128,128]{2,1,0:T(8,128)(2,1)} %bitcast.9, bf16[8,128,128]{2,1,0:T(8,128)(2,1)} %bitcast.10, bf16[8,128,128]{2,1,0:T(8,128)(2,1)} %bitcast.11), custom_call_target="tpu_custom_call" | custom-call | tf_op jit(solution)/shard_map/hessian/pallas_call | solution.py:519
  127.6 0.7 copy.9

commit v6 on v5

--- a/solution.py
+++ b/solution.py
@@ -16,7 +16,7 @@
     cols_hbm, step, inter, dens, fock_hbm, out, trace,
     cols, fock, in_sem,
     r_i, r_d, r_k, l_p, l_s, l_c, parts, landed, own, x_send, x_recv0, x_recv1, t_src, t_buf, pick, tpick,
-    p1_send, p1_recv_a, p1_recv_b, p1_local, p2_send, p2_recv_a, p2_recv_b,
+    p1_send, p1_fsend, p1_recv_a, p1_recv_b, p1_local, p2_send, p2_recv_a, p2_recv_b,
     l_send, l_recv, l_local, rs_send, rs_recv, x_ssem, x_rsem, x_local, relay, rl_ssem, rl_rsem, rl_fsem, t_send, t_recv,
 ):
     cols_copy = pltpu.make_async_copy(cols_hbm, cols, in_sem.at[0])
@@ -59,72 +59,110 @@
 
     gathers = ((inter, r_i), (dens, r_d), (fock_hbm, r_k))
 
-    def p1_copy(m, d):
+    def p1_copy(m, kind, off, half):
         tile, buf = gathers[m]
-        slot_a = (y * 2 + zz) * 8
-        slot_b = (8 + zz * 4 + y) * 8
-        kind, off = d
+        ssem = p1_send.at[m, off * 2 + half]
+        part = tile.at[pl.ds(half * 4, 4)]
         if kind == "a":
-            return remote(tile, buf.at[pl.ds(slot_a, 8)], p1_send.at[m, off], p1_recv_a.at[m, zz], dev(x, h, y, (z + off) % 4))
-        return remote(tile, buf.at[pl.ds(slot_b, 8)], p1_send.at[m, off], p1_recv_b.at[m, y], dev(x, h, (y + off) % 4, z))
+            slot = buf.at[pl.ds((y * 2 + zz) * 8 + half * 4, 4)]
+            return remote(part, slot, ssem, p1_recv_a.at[m, zz, half], dev(x, h, y, (z + off) % 4))
+        slot = buf.at[pl.ds((8 + zz * 4 + y) * 8 + half * 4, 4)]
+        return remote(part, slot, ssem, p1_recv_b.at[m, y, half], dev(x, h, (y + off) % 4, z))
 
     def p1_local_copy(m):
         tile, buf = gathers[m]
         slot = jnp.where(k == 0, y * 2 + zz, 8 + zz * 4 + y) * 8
         return pltpu.make_async_copy(tile, buf.at[pl.ds(slot, 8)], p1_local.at[m])
 
+    p1_own = ((0, 1), (1, 3), (1, 1), (0, 3), (0, 0), (1, 0))
+    p1_fwd = ((0, 1), (1, 3))
+
+    def p1_each(m, act):
+        for half, off in p1_own:
+            go = (k != h) if off == 0 else True
+
+            @pl.when((k == 0) & go)
+            def _():
+                act(p1_copy(m, "a", off, half))
+
+            @pl.when((k == 1) & go)
+            def _():
+                act(p1_copy(m, "b", off, half))
+
     def p1_start(m):
-        for off in (1, 3, 2, 0):
-            go = (k != h) if off == 0 else True
-
-            @pl.when((k == 0) & go)
-            def _():
-                p1_copy(m, ("a", off)).start()
-
-            @pl.when((k == 1) & go)
-            def _():
-                p1_copy(m, ("b", off)).start()
+        p1_each(m, lambda c: c.start())
 
         @pl.when(k == h)
         def _():
             p1_local_copy(m).start()
 
+    def near(off):
+        return (z + 4 - off) % 4 // 2 == k
+
+    def slot_a(off):
+        return (y * 2 + (z + 4 - off) % 2) * 8
+
+    def slot_b(off):
+        return (8 + zz * 4 + (y + 4 - off) % 4) * 8
+
+    def p1_fwd_a(m, half, off):
+        buf = gathers[m][1]
+        view = buf.at[pl.ds(slot_a(off) + half * 4, 4)]
+        q = (z + 4 - off) % 2
+        return remote(view, view, p1_fsend.at[m, 0, half], p1_recv_a.at[m, q, half], dev(x, k, y, (z + off) % 4))
+
+    def p1_fwd_b(m, half, off):
+        buf = gathers[m][1]
+        view = buf.at[pl.ds(slot_b(off) + half * 4, 4)]
+        src = (y + 4 - off) % 4
+        return remote(view, view, p1_fsend.at[m, 1, half], p1_recv_b.at[m, src, half], dev(x, k, (y + off) % 4, z))
+
+    def p1_get_a(m, off, half):
+        recv_wait(gathers[m][1], slot_a(off) + half * 4, 4, p1_recv_a.at[m, (z + 4 - off) % 2, half])
+
+    def p1_get_b(m, off, half):
+        recv_wait(gathers[m][1], slot_b(off) + half * 4, 4, p1_recv_b.at[m, (y + 4 - off) % 4, half])
+
+    def p1_relay(m):
+        for half, off in p1_fwd:
+            @pl.when(near(off))
+            def _():
+                p1_get_a(m, off, half)
+                p1_fwd_a(m, half, off).start()
+
+            @pl.when(k == h)
+            def _():
+                p1_get_b(m, off, half)
+                p1_fwd_b(m, half, off).start()
+
     def p1_wait_send(m):
-        for off in (1, 3, 2, 0):
-            go = (k != h) if off == 0 else True
-
-            @pl.when((k == 0) & go)
-            def _():
-                p1_copy(m, ("a", off)).wait_send()
-
-            @pl.when((k == 1) & go)
-            def _():
-                p1_copy(m, ("b", off)).wait_send()
+        p1_each(m, lambda c: c.wait_send())
+        for half, off in p1_fwd:
+            @pl.when(near(off))
+            def _():
+                p1_fwd_a(m, half, off).wait_send()
+
+            @pl.when(k == h)
+            def _():
+                p1_fwd_b(m, half, off).wait_send()
 
     def recv_wait(buf, start, n, sem):
         view = buf.at[pl.ds(start, n)]
         remote(view, view, sem, sem, dev(x, 1 - k, y, z)).wait_recv()
 
     def p1_wait(m):
-        tile, buf = gathers[m]
-
         @pl.when(k == h)
         def _():
             p1_local_copy(m).wait()
 
-        for q in range(2):
-            mine = (k == 0) & (h == 0) & (zz == q)
-
-            @pl.when(jnp.logical_not(mine))
-            def _():
-                recv_wait(buf, (y * 2 + q) * 8, 8, p1_recv_a.at[m, q])
-
-        for yy in range(4):
-            mine = (k == 1) & (y == yy)
-
-            @pl.when((k == h) & jnp.logical_not(mine))
-            def _():
-                recv_wait(buf, (8 + zz * 4 + yy) * 8, 8, p1_recv_b.at[m, yy])
+        for off, half in ((1, 1), (3, 0), (2, 0), (2, 1), (0, 0), (0, 1)):
+            @pl.when(near(off) & ((k != 0) if off == 0 else True))
+            def _():
+                p1_get_a(m, off, half)
+
+            @pl.when((k == h) & ((k != 1) if off == 0 else True))
+            def _():
+                p1_get_b(m, off, half)
 
     def p2_a(m, src, half, off, fwd):
         buf = gathers[m][1]
@@ -153,9 +191,6 @@
 
     def p2_wait_b(m, q, half):
         recv_wait(gathers[m][1], 64 + q * 32 + half * 16, 16, p2_recv_b.at[m, q, half])
-
-    def near(off):
-        return (z + 4 - off) % 4 // 2 == k
 
     def p2_relay(m):
         for half, off in ways[:2]:
@@ -210,6 +245,8 @@
     p1_start(0)
     for c in range(2):
         l_swap(0, step, l_p, c).start()
+
+    p1_relay(0)
     p1_start(1)
 
     base = row * 4
@@ -251,6 +288,7 @@
 
     p1_wait(0)
     p2_start(0)
+    p1_relay(1)
     p2_relay(0)
     p1_wait(1)
     p2_start(1)
@@ -402,6 +440,7 @@
         if c == 0:
             p2_relay(1)
             p1_start(2)
+    p1_relay(2)
     l_wait(1, l_s.at[k], l_s)
     p2_wait(1)
 
@@ -529,7 +568,7 @@
             pltpu.VMEM((2, 8) + blk, BF), pltpu.VMEM((17,) + blk, BF), pltpu.VMEM((17,) + blk, BF),
             pltpu.VMEM((3, 8, 128), F32), pltpu.VMEM((3, 8, 8, 128), F32),
             pltpu.SMEM((128,), jnp.int32), pltpu.SMEM((8,), jnp.int32),
-            dma((3, 4)), dma((3, 2)), dma((3, 4)), dma((3,)), dma((3, 2, 8)), dma((3, 4, 2)), dma((3, 2, 2)),
+            dma((3, 8)), dma((3, 2, 2)), dma((3, 2, 2)), dma((3, 4, 2)), dma((3,)), dma((3, 2, 8)), dma((3, 4, 2)), dma((3, 2, 2)),
             dma((3, 2)), dma((3, 2)), dma((1,)), dma((3, 4, 2)), dma((3, 4, 2)), dma((2, 2, 2)), dma((2, 2)), dma((2, 2)),
             pltpu.VMEM((2, 4, 8) + blk, BF), dma((2, 2)), dma((2, 4, 2)), dma((2, 4, 4)),
             dma((3, 8)), dma((3, 8)),

time: 130 us -> 131 us (level)
  no operation moved by 1% of the time
where the time goes in v6:
time: 131 us
  Pallas kernels  128 us (98%)
  between operations  2.33 us (2%)
    pallas_call x1, Pallas kernels, per_device(): pl.pallas_call(kernel, out_shape=(pltpu.VMEM((8, 128, 128), BF), jax.Shap...  128 us

profile of v6, /device:TPU:39, one launch (start us, length us, event | category | flops | bytes accessed | tf_op | source)
XLA Modules:
  0.0 130.8 jit_solution(1639888090907351856)
XLA Ops:
  0.6 127.7 %hessian.1 = (bf16[8,128,128]{2,1,0:T(8,128)(2,1)S(1)}, f32[1,1]{1,0:T(1,128)}) custom-call(s32[16,64]{1,0:T(8,128)} %bitcast.12, bf16[8,128,128]{2,1,0:T(8,128)(2,1)} %bitcast.8, bf16[8,128,128]{2,1,0:T(8,128)(2,1)} %bitcast.9, bf16[8,128,128]{2,1,0:T(8,128)(2,1)} %bitcast.10, bf16[8,128,128]{2,1,0:T(8,128)(2,1)} %bitcast.11), custom_call_target="tpu_custom_call" | custom-call | tf_op jit(solution)/shard_map/hessian/pallas_call | solution.py:558
  128.4 0.7 copy.9
